TPU v7x, 256 devices: a whole 4x4x8 slice. The times are simulated.
256 devices in a mesh: loop: 32 (over z, x_lo, core), group: 8 (over y, x_hi).
Axes of the slice: x: 4 (x_hi: 2, x_lo: 2; x = x_hi * 2 + x_lo), y: 4, z: 8, core: 2. Of those that a mesh axis runs over, the one named last changes fastest.
Arguments:
- images: bfloat16 [8, 256, 7, 7, 1536], P('group', 'loop'), as said below
- targets: int32 [8, 256], P('group'), may hold values from 0 to 131071, as said below
- kernel: bfloat16 [7, 7, 1536], replicated, may hold values from -0.875 to 0.875
- projection: bfloat16 [1536, 768], replicated, as said below
- captions: bfloat16 [131072, 768], P('loop'), as said below
Outputs:
- loss: float32 [8, 256], P('group', 'loop')
- image_grad: bfloat16 [8, 256, 7, 7, 1536], P('group', 'loop')
- kernel_grad: float32 [1536, 49], P(('loop', 'group'))
Inputs may be any that keep to these rules, and one draw needn't show every extreme that they name: targets index captions of the whole gallery. `images`: finite real values. `projection`: finite real values. `captions`: finite real values, no caption all zero.
All inputs are finite; a program needn't handle non-finite values.
Results may differ from a plain program's by a relative error of at most 0.0066.
Values may be sent and summed in bfloat16 or wider, within the bound.
A program may use at most 64 MiB of HBM per device.

v0:
```python
import jax
import jax.numpy as jnp
from jax import lax
from jax.sharding import PartitionSpec as P

logit_sharpness = 20.0


def depthwise(padded, kernel):
    reach = kernel.shape[0]
    side = padded.shape[1] - reach + 1
    total = jnp.zeros((padded.shape[0], side, side, padded.shape[3]), jnp.float32)
    for row_off in range(reach):
        for col_off in range(reach):
            window = padded[:, row_off : row_off + side, col_off : col_off + side, :].astype(
                jnp.float32
            )
            total = total + window * kernel[row_off, col_off].astype(jnp.float32)
    return total


def forward(pixels, kernel, projection):
    margin = kernel.shape[0] // 2
    padded = jnp.pad(pixels, ((0, 0), (margin, margin), (margin, margin), (0, 0)))
    hidden = depthwise(padded, kernel)
    centre = hidden - jnp.mean(hidden, -1, keepdims=True)
    scale_inv = lax.rsqrt(jnp.mean(centre * centre, -1, keepdims=True) + 1e-06)
    normed = centre * scale_inv
    pooled = jnp.mean(pixels.astype(jnp.float32) + normed, axis=(1, 2)).astype(jnp.bfloat16)
    embedded = jnp.dot(pooled, projection, preferred_element_type=jnp.float32)
    inv_norm = lax.rsqrt(jnp.sum(embedded * embedded, -1, keepdims=True) + 1e-06)
    return (padded, normed, scale_inv, embedded, inv_norm)


def backward(padded, normed, scale_inv, embedded, inv_norm, kernel, projection, query_gradient):
    unit = embedded * inv_norm
    emb_grad = (
        (query_gradient - unit * jnp.sum(unit * query_gradient, -1, keepdims=True)) * inv_norm
    ).astype(jnp.bfloat16)
    pooled_grad = lax.dot_general(
        emb_grad, projection, (((1,), (1,)), ((), ())), preferred_element_type=jnp.float32
    )
    side = normed.shape[1]
    out_grad = (pooled_grad / (side * side))[:, None, None, :]
    hidden_grad = scale_inv * (
        out_grad
        - jnp.mean(out_grad, -1, keepdims=True)
        - normed * jnp.mean(normed * out_grad, -1, keepdims=True)
    )
    reach = kernel.shape[0]
    margin = reach // 2
    grad_pad = jnp.pad(hidden_grad, ((0, 0), (margin, margin), (margin, margin), (0, 0)))
    input_grad = out_grad + depthwise(grad_pad, kernel[::-1, ::-1])
    taps = []
    for row_off in range(reach):
        for col_off in range(reach):
            window = padded[:, row_off : row_off + side, col_off : col_off + side, :].astype(
                jnp.float32
            )
            taps.append(jnp.sum(window * hidden_grad, axis=(0, 1, 2)))
    return (input_grad, jnp.stack(taps, 0).T)


def normalize(captions):
    values = captions.astype(jnp.float32)
    return (values * lax.rsqrt(jnp.sum(values * values, -1, keepdims=True) + 1e-06)).astype(
        jnp.bfloat16
    )


def shards(images, targets, kernel, projection, captions):
    pixels = images[0]
    group_targets = targets[0]
    own_rows = pixels.shape[0]
    cap_rows = captions.shape[0]
    group_rows = group_targets.shape[0]
    padded, normed, scale_inv, embedded, inv_norm = forward(pixels, kernel, projection)
    query = (embedded * inv_norm).astype(jnp.bfloat16)
    normalized_caption_vectors = normalize(captions)
    similarity_scores = logit_sharpness * lax.dot_general(
        lax.all_gather(query, "loop", axis=0, tiled=True),
        normalized_caption_vectors,
        (((1,), (1,)), ((), ())),
        preferred_element_type=jnp.float32,
    )
    col_part = jnp.sum(jnp.exp(similarity_scores), 0)
    col_log = jnp.log(lax.psum(col_part, "group"))
    weight = jnp.exp(similarity_scores - col_log)
    local_index = group_targets - lax.axis_index("loop") * cap_rows
    onehot = (
        local_index[:, None] == lax.broadcasted_iota(jnp.int32, (group_rows, cap_rows), 1)
    ).astype(jnp.float32)
    row_part = jnp.sum(weight, 1)
    target_part = jnp.sum(onehot * (similarity_scores - col_log), 1)
    row_sum, target_logit = lax.psum((row_part, target_part), "loop")
    loss_group = jnp.log(row_sum) - target_logit
    own_start = lax.axis_index("loop") * own_rows
    own_loss = lax.dynamic_slice_in_dim(loss_group, own_start, own_rows, 0)
    grad = weight / row_sum[:, None] - onehot
    col_grad = lax.psum(jnp.sum(grad, 0), "group")
    similarity_gradient = (grad - weight * col_grad).astype(jnp.bfloat16)
    incomplete_gradient = logit_sharpness * jnp.dot(
        similarity_gradient, normalized_caption_vectors, preferred_element_type=jnp.float32
    )
    summed = lax.psum(incomplete_gradient, "loop")
    query_gradient = lax.dynamic_slice_in_dim(summed, own_start, own_rows, 0)
    input_grad, kernel_terms = backward(
        padded, normed, scale_inv, embedded, inv_norm, kernel, projection, query_gradient
    )
    kernel_share = lax.psum_scatter(
        kernel_terms, ("loop", "group"), scatter_dimension=0, tiled=True
    )
    return (own_loss[None], input_grad.astype(jnp.bfloat16)[None], kernel_share)


def solution(mesh):
    placed = (P("group", "loop", None, None, None), P("group", None), P(), P(), P("loop", None))
    return jax.shard_map(
        shards,
        mesh=mesh,
        in_specs=placed,
        out_specs=(
            P("group", "loop"),
            P("group", "loop", None, None, None),
            P(("loop", "group"), None),
        ),
        check_vma=False,
    )
```

profile of v0, /device:TPU:1, one launch (start us, length us, event | category | flops | bytes accessed | tf_op | source)
XLA Modules:
  0.0 739.3 jit_solution(11930092785954452918)
XLA Ops:
  7.2 0.0 copy-start
  7.2 0.0 all-reduce.6.cloned.1.call-start
  7.2 1.2 convert_reduce_fusion.46
  8.5 1.5 convert_reduce_fusion.48
  10.0 1.6 convert_reduce_fusion.47
  11.6 0.0 copy-start.3
  11.6 31.9 %fusion.216 = (f32[8,7,7]{0,2,1:T(8,128)S(1)}, f32[8,7,7,1536]{3,0,2,1:T(8,128)S(1)}) fusion(f32[1536]{0:T(1024)S(1)} %get-tuple-element.107, f32[1536]{0:T(1024)S(1)} %get-tuple-element.108, f32[1536]{0:T(1024)S(1)} %get-tuple-element.61, f32[1536]{0:T(1024)S(1)} %get-tuple-element.62, f32[1536]{0:T(1024)S(1)} %get-tuple-element.63, ...), kind=kLoop, calls=%fused_computation.486 | loop fusion | flops 88510072 | bytes 3915296 | tf_op jit(solution)/shard_map/reduce_sum | solution.py:26
  43.5 0.0 copy-start.1
  43.5 0.4 multiply_reduce_fusion.1
  43.9 0.0 copy-done.3
  43.9 0.0 copy-start.6
  43.9 0.5 fusion.103
  44.4 0.5 copy-done.1
  44.9 0.0 copy-done
  44.9 0.5 multiply_reduce_fusion.3
  45.5 0.1 multiply_convert_fusion.3
  45.6 39.6 %all_gather.3 = bf16[256,768]{1,0:T(8,128)(2,1)S(1)} all-gather(bf16[8,768]{1,0:T(8,128)(2,1)S(1)} %multiply_convert_fusion.3), channel_id=1, replica_groups=mesh['loop'=32,'group'=8] {'loop'}, dimensions={0}, use_global_device_ids=true | all-gather | bytes 405504 | tf_op jit(solution)/shard_map/all_gather | solution.py:81
  85.2 0.0 copy-done.6
  85.2 1.3 fusion
  86.5 3.8 exponential_reduce_fusion
  90.4 34.7 %psum.35 = f32[4096]{0:T(1024)S(1)} all-reduce(f32[4096]{0:T(1024)S(1)} %get-tuple-element.114), channel_id=1, replica_groups=mesh['loop'=32,'group'=8] {'group'}, use_global_device_ids=true, to_apply=%region_6.7 | all-reduce | flops 4096 | bytes 32768 | tf_op jit(solution)/shard_map/psum | solution.py:87
  125.1 2.8 fusion.3
  127.9 59.8 %psum.36 = f32[256]{0:T(256)S(1)} all-reduce(f32[256]{0:T(256)S(1)} %fusion.3), channel_id=1, replica_groups=mesh['loop'=32,'group'=8] {'loop'}, use_global_device_ids=true, to_apply=%region_8.9 | all-reduce | flops 256 | bytes 2048 | tf_op jit(solution)/shard_map/psum | solution.py:95
  187.7 0.0 copy-done.7
  187.7 4.2 fusion.2
  191.9 30.1 %psum.38 = f32[4096]{0:T(1024)S(1)} all-reduce(f32[4096]{0:T(1024)S(1)} %get-tuple-element.9), channel_id=1, replica_groups=mesh['loop'=32,'group'=8] {'group'}, use_global_device_ids=true, to_apply=%region_12.13 | all-reduce | flops 4096 | bytes 32768 | tf_op jit(solution)/shard_map/psum | solution.py:100
  222.0 8.0 %fusion.206 = f32[256,768]{1,0:T(8,128)} fusion(bf16[4096,768]{1,0:T(8,128)(2,1)} %param.9, f32[4096]{0:T(1024)S(1)} %add_rsqrt_fusion.1, f32[256,4096]{1,0:T(8,128)} %get-tuple-element.115, f32[4096]{0:T(1024)S(1)} %psum.38, f32[256]{0:T(256)S(1)} %psum.36, s32[256]{0:T(256)S(1)} %bitcast.20, f32[4096]{0:T(1024)S(1)} %log.6), kind=kOutput, calls=%fused_computation.413 | convolution fusion | flops 1628635136 | bytes 11323392 | tf_op jit(solution)/shard_map/dot_general | solution.py:102
  230.0 0.0 all-reduce.6.cloned.1.call-update
  230.0 0.0 all-reduce.8.cloned.1.call-start
  230.1 59.9 %psum.37 = f32[256]{0:T(256)S(1)} all-reduce(f32[256]{0:T(256)S(1)} %get-tuple-element.10), channel_id=1, replica_groups=mesh['loop'=32,'group'=8] {'loop'}, use_global_device_ids=true, to_apply=%region_10.11 | all-reduce | flops 256 | bytes 2048 | tf_op jit(solution)/shard_map/psum | solution.py:95
  290.0 0.6 dynamic-slice_bitcast_fusion
  290.6 167.9 %all-reduce.6.cloned.1.call-done = f32[256,768]{1,0:T(8,128)} async-done(((f32[256,768]{1,0:T(8,128)}), f32[256,768]{1,0:T(8,128)}) %all-reduce.6.cloned.1.call-update) | async-done | bytes 786448 | tf_op jit(solution)/shard_map/psum | solution.py:105
  458.5 1.1 multiply_reduce_fusion.2
  459.6 1.7 fusion.218
  461.3 0.0 copy-done.2
  461.3 0.5 multiply_reduce_fusion
  461.8 0.1 broadcast_subtract_fusion
  461.8 0.0 copy-done.4
  461.8 7.7 %fusion.102 = (f32[1536]{0:T(1024)S(1)}, f32[1536]{0:T(1024)S(1)}, f32[1536]{0:T(1024)S(1)}, f32[1536]{0:T(1024)S(1)}, f32[1536]{0:T(1024)S(1)}, /*index=5*/f32[...) fusion(bf16[8,7,7,1536]{3,0,2,1:T(8,128)(2,1)S(1)} %bitcast.15,, ...), kind=kLoop, calls=%fused_computation.304 | loop fusion | flops 35496960 | bytes 6185568 | tf_op jit(solution)/shard_map/reduce_sum | solution.py:60
  469.6 0.0 copy-start.5
  469.6 2.3 fusion.43
  472.0 3.5 fusion.84
  476.2 4.8 stack.199
  480.9 0.0 all-reduce.8.cloned.1.call-update
  481.0 38.0 %fusion.209 = bf16[1,8,7,7,1536]{4,1,3,2,0:T(8,128)(2,1)} fusion(f32[1536]{0:T(1024)S(1)} %get-tuple-element.60, f32[8,7,7,1536]{3,0,2,1:T(8,128)} %copy-done.5, f32[1536]{0:T(1024)S(1)} %get-tuple-element.79, f32[1536]{0:T(1024)S(1)} %get-tuple-element.98, f32[1536]{0:T(1024)S(1)} %get-tuple-element.106, f32[1536]{0:T(1024)S(1)} %get-tuple-element.105, ...), kind=kLoop, calls=%fused_computation.414 | loop fusion | flops 59609088 | bytes 3962880 | tf_op jit(solution)/shard_map/broadcast_in_dim | solution.py:113
  519.0 211.9 %all-reduce.8.cloned.1.call-done = f32[1536,49]{0,1:T(8,128)} async-done(((f32[1536,49]{0,1:T(8,128)}), f32[1536,49]{0,1:T(8,128)}) %all-reduce.8.cloned.1.call-update) | async-done | bytes 301072
  730.9 0.9 constant_dynamic-slice_fusion
  731.7 0.7 copy.9
  (62 shorter events, 0.4 us)
Async XLA Ops:
  7.2 37.8 %copy-start = (bf16[1536,768]{1,0:T(8,128)(2,1)S(1)}, bf16[1536,768]{1,0:T(8,128)(2,1)}, u32[]{:S(2)}) copy-start(bf16[1536,768]{1,0:T(8,128)(2,1)} %param.8) | copy-start | bytes 7077892
  7.2 451.3 %all-reduce.6.cloned.1.call-start = ((), (), s32[]{:S(2)}) async-start(), calls=%async_computation | async-start | bytes 1572864 | tf_op jit(solution)/shard_map/psum | solution.py:105
  11.6 32.3 %copy-start.3 = (bf16[1,8,7,7,1536]{4,1,3,2,0:T(8,128)(2,1)S(1)}, bf16[1,8,7,7,1536]{4,1,3,2,0:T(8,128)(2,1)}, u32[]{:S(2)}) copy-start(bf16[1,8,7,7,1536]{4,1,3,2,0:T(8,128)(2,1)} %param.5) | copy-start | bytes 3612676
  43.5 1.5 copy-start.1
  43.9 41.3 %copy-start.6 = (bf16[4096,768]{1,0:T(8,128)(2,1)S(1)}, bf16[4096,768]{1,0:T(8,128)(2,1)}, u32[]{:S(2)}) copy-start(bf16[4096,768]{1,0:T(8,128)(2,1)} %param.9) | copy-start | bytes 18874372
  90.4 97.4 %copy-start.7 = (s32[1,256]{1,0:T(1,128)S(1)}, s32[1,256]{1,0:T(1,128)}, u32[]{:S(2)}) copy-start(s32[1,256]{1,0:T(1,128)} %param.6) | copy-start | bytes 3076
  230.0 500.8 %all-reduce.8.cloned.1.call-start = ((), (), s32[]{:S(2)}) async-start(), calls=%async_computation.1 | async-start | bytes 688128
  458.5 2.8 copy-start.2
  459.6 2.3 copy-start.4
  469.6 2.4 copy-start.5
Sparse Core Ops, SparseCore 0:
  230.1 228.3 all-reduce.5
  481.1 249.7 all-reduce.7
where the time goes:
time: 740 us; the launch traced here: 739 us
  waiting for transfers between devices  380 us (51%)
  blocking collectives  224 us (30%)
  other arithmetic  98.7 us (13%)
  between operations  14.6 us (2%)
  matrix products  14.1 us (2%)
  local copies, waits for them, and re-layouts  7.81 us (1%)
    unnamed x3, waiting for transfers between devices  212 us
    psum x1, waiting for transfers between devices, shards(): summed = lax.psum(incomplete_gradient, 'loop')  168 us
    psum x2, blocking collectives, shards(): row_sum, target_logit = lax.psum((row_part, target_part), 'loop')  120 us
    all_gather x1, blocking collectives, shards(): lax.all_gather(query, 'loop', axis=0, tiled=True)  39.6 us
    broadcast_in_dim x1, other arithmetic, shards(): return (own_loss[None], input_grad.astype(jnp.bfloat16)[None], kernel_share)  38 us
    psum x1, blocking collectives, shards(): col_log = jnp.log(lax.psum(col_part, 'group'))  34.7 us
    reduce_sum x1, other arithmetic, forward(): centre = hidden - jnp.mean(hidden, -1, keepdims=True)  31.9 us
    psum x1, blocking collectives, shards(): col_grad = lax.psum(jnp.sum(grad, 0), 'group')  30.1 us
  transfers between devices with their start and end apart: 2, of which 2 were waited for; matrix products, arithmetic and copies ran while one was open for 5% of the time, Pallas kernels for 0%

commit v1 on v0

--- a/solution.py
+++ b/solution.py
@@ -78,7 +78,9 @@
     query = (embedded * inv_norm).astype(jnp.bfloat16)
     normalized_caption_vectors = normalize(captions)
     similarity_scores = logit_sharpness * lax.dot_general(
-        lax.all_gather(query, "loop", axis=0, tiled=True),
+        jnp.concatenate(
+            lax.all_to_all(jnp.stack([query] * lax.axis_size("loop")), "loop", 0, 0), axis=0
+        ),
         normalized_caption_vectors,
         (((1,), (1,)), ((), ())),
         preferred_element_type=jnp.float32,

time: 740 us -> 729 us (0.985)
  blocking collectives: 224 us -> 186 us
  starting transfers between devices: 0.08 us -> 11.1 us
  waiting for transfers between devices: 380 us -> 389 us
    all_gather x1 -> x0, blocking collectives: 39.6 us -> none  [shards(): lax.all_gather(query, 'loop', axis=0, tiled=True)]
    all_to_all x0 -> x1, starting transfers between devices: none -> 11 us  [shards(): lax.all_to_all(jnp.stack([query] * lax.axis_size('loop')), 'loop', 0, 0)]
    all_to_all x0 -> x1, waiting for transfers between devices: none -> 9.55 us  [shards(): lax.all_to_all(jnp.stack([query] * lax.axis_size('loop')), 'loop', 0, 0)]
  transfers between devices with their start and end apart: 2 -> 3, of which waited for: 2 -> 3; matrix products, arithmetic and copies ran while one was open for 5% -> 6% of each run, Pallas kernels for 0% -> 0%
where the time goes in v1:
time: 729 us; the launch traced here: 728 us
  waiting for transfers between devices  389 us (53%)
  blocking collectives  186 us (26%)
  other arithmetic  102 us (14%)
  matrix products  17.1 us (2%)
  between operations  14.6 us (2%)
  starting transfers between devices  11.1 us (2%)
  local copies, waits for them, and re-layouts  8.6 us (1%)
    unnamed x3, waiting for transfers between devices  212 us
    psum x1, waiting for transfers between devices, shards(): summed = lax.psum(incomplete_gradient, 'loop')  168 us
    psum x2, blocking collectives, shards(): row_sum, target_logit = lax.psum((row_part, target_part), 'loop')  121 us
    broadcast_in_dim x1, other arithmetic, shards(): return (own_loss[None], input_grad.astype(jnp.bfloat16)[None], kernel_share)  38.3 us
    psum x1, blocking collectives, shards(): col_log = jnp.log(lax.psum(col_part, 'group'))  34.8 us
    reduce_sum x1, other arithmetic, forward(): centre = hidden - jnp.mean(hidden, -1, keepdims=True)  31.9 us
    psum x1, blocking collectives, shards(): col_grad = lax.psum(jnp.sum(grad, 0), 'group')  30.1 us
  transfers between devices with their start and end apart: 3, of which 3 were waited for; matrix products, arithmetic and copies ran while one was open for 6% of the time, Pallas kernels for 0%

profile of v1, /device:TPU:1, one launch (start us, length us, event | category | flops | bytes accessed | tf_op | source)
XLA Modules:
  0.0 728.1 jit_solution(10695760108254949127)
XLA Ops:
  7.2 0.0 copy-start
  7.2 1.2 convert_reduce_fusion.46
  8.4 1.5 convert_reduce_fusion.48
  9.9 1.6 convert_reduce_fusion.47
  11.5 0.0 copy-start.3
  11.5 31.9 %fusion.217 = (f32[8,7,7]{0,2,1:T(8,128)S(1)}, f32[8,7,7,1536]{3,0,2,1:T(8,128)S(1)}) fusion(f32[1536]{0:T(1024)S(1)} %get-tuple-element.107, f32[1536]{0:T(1024)S(1)} %get-tuple-element.108, f32[1536]{0:T(1024)S(1)} %get-tuple-element.61, f32[1536]{0:T(1024)S(1)} %get-tuple-element.62, f32[1536]{0:T(1024)S(1)} %get-tuple-element.63, ...), kind=kLoop, calls=%fused_computation.487 | loop fusion | flops 88510072 | bytes 3915296 | tf_op jit(solution)/shard_map/reduce_sum | solution.py:26
  43.4 0.0 copy-start.1
  43.4 0.4 multiply_reduce_fusion.1
  43.8 0.0 copy-done.3
  43.9 0.5 fusion.103
  44.3 0.6 copy-done.1
  44.9 0.0 copy-done
  44.9 0.5 multiply_reduce_fusion.3
  45.4 0.1 multiply_convert_fusion.3
  45.5 0.8 stack.185
  46.3 11.0 %all-to-all-start = ((bf16[32,8,768]{2,1,0:T(8,128)(2,1)}), bf16[32,8,768]{2,1,0:T(8,128)(2,1)S(1)}, u32[]{:S(2)}, u32[]{:S(2)}) async-start(bf16[32,8,768]{2,1,0:T(8,128)(2,1)} %stack.185), calls=%async_computation | async-start | bytes 786432 | tf_op jit(solution)/shard_map/all_to_all | solution.py:82
  57.3 0.0 all-reduce.6.cloned.1.call-start
  57.4 0.0 copy-done.6
  57.4 4.1 fusion
  61.5 9.6 %all-to-all-done = bf16[32,8,768]{2,1,0:T(8,128)(2,1)S(1)} async-done(((bf16[32,8,768]{2,1,0:T(8,128)(2,1)}), bf16[32,8,768]{2,1,0:T(8,128)(2,1)S(1)}, u32[]{:S(2)}, u32[]{:S(2)}) %all-to-all-start) | async-done | bytes 393248 | tf_op jit(solution)/shard_map/all_to_all | solution.py:82
  71.1 6.9 exponential_reduce_fusion
  77.9 34.8 %psum.35 = f32[4096]{0:T(1024)S(1)} all-reduce(f32[4096]{0:T(1024)S(1)} %get-tuple-element.114), channel_id=1, replica_groups=mesh['loop'=32,'group'=8] {'group'}, use_global_device_ids=true, to_apply=%region_6.7 | all-reduce | flops 4096 | bytes 32768 | tf_op jit(solution)/shard_map/psum | solution.py:89
  112.7 2.9 fusion.3
  115.6 61.3 %psum.36 = f32[256]{0:T(256)S(1)} all-reduce(f32[256]{0:T(256)S(1)} %fusion.3), channel_id=1, replica_groups=mesh['loop'=32,'group'=8] {'loop'}, use_global_device_ids=true, to_apply=%region_8.9 | all-reduce | flops 256 | bytes 2048 | tf_op jit(solution)/shard_map/psum | solution.py:97
  176.9 4.2 fusion.2
  181.1 30.1 %psum.38 = f32[4096]{0:T(1024)S(1)} all-reduce(f32[4096]{0:T(1024)S(1)} %get-tuple-element.9), channel_id=1, replica_groups=mesh['loop'=32,'group'=8] {'group'}, use_global_device_ids=true, to_apply=%region_12.13 | all-reduce | flops 4096 | bytes 32768 | tf_op jit(solution)/shard_map/psum | solution.py:102
  211.2 8.0 %fusion.206 = f32[256,768]{1,0:T(8,128)} fusion(bf16[4096,768]{1,0:T(8,128)(2,1)} %param.9, f32[4096]{0:T(1024)S(1)} %add_rsqrt_fusion.1, f32[256,4096]{1,0:T(8,128)} %get-tuple-element.115, f32[4096]{0:T(1024)S(1)} %psum.38, f32[256]{0:T(256)S(1)} %psum.36, s32[256]{0:T(256)S(1)} %bitcast.24, f32[4096]{0:T(1024)S(1)} %log.6), kind=kOutput, calls=%fused_computation.413 | convolution fusion | flops 1628635136 | bytes 11323392 | tf_op jit(solution)/shard_map/dot_general | solution.py:104
  219.2 0.0 all-reduce.6.cloned.1.call-update
  219.2 0.0 all-reduce.8.cloned.1.call-start
  219.3 59.7 %psum.37 = f32[256]{0:T(256)S(1)} all-reduce(f32[256]{0:T(256)S(1)} %get-tuple-element.10), channel_id=1, replica_groups=mesh['loop'=32,'group'=8] {'loop'}, use_global_device_ids=true, to_apply=%region_10.11 | all-reduce | flops 256 | bytes 2048 | tf_op jit(solution)/shard_map/psum | solution.py:97
  279.1 0.6 dynamic-slice_bitcast_fusion
  279.6 167.8 %all-reduce.6.cloned.1.call-done = f32[256,768]{1,0:T(8,128)} async-done(((f32[256,768]{1,0:T(8,128)}), f32[256,768]{1,0:T(8,128)}) %all-reduce.6.cloned.1.call-update) | async-done | bytes 786448 | tf_op jit(solution)/shard_map/psum | solution.py:107
  447.4 1.1 multiply_reduce_fusion.2
  448.5 1.7 fusion.219
  450.2 0.0 copy-done.2
  450.2 0.5 multiply_reduce_fusion
  450.7 0.1 broadcast_subtract_fusion
  450.8 0.0 copy-done.4
  450.8 7.7 %fusion.102 = (f32[1536]{0:T(1024)S(1)}, f32[1536]{0:T(1024)S(1)}, f32[1536]{0:T(1024)S(1)}, f32[1536]{0:T(1024)S(1)}, f32[1536]{0:T(1024)S(1)}, /*index=5*/f32[...) fusion(bf16[8,7,7,1536]{3,0,2,1:T(8,128)(2,1)S(1)} %bitcast.19,, ...), kind=kLoop, calls=%fused_computation.304 | loop fusion | flops 35496960 | bytes 6185568 | tf_op jit(solution)/shard_map/reduce_sum | solution.py:60
  458.5 0.0 copy-start.5
  458.5 2.3 fusion.43
  460.8 3.5 fusion.84
  465.0 4.8 stack.235
  469.8 0.0 all-reduce.8.cloned.1.call-update
  469.8 38.3 %fusion.209 = bf16[1,8,7,7,1536]{4,1,3,2,0:T(8,128)(2,1)} fusion(f32[1536]{0:T(1024)S(1)} %get-tuple-element.60, f32[8,7,7,1536]{3,0,2,1:T(8,128)} %copy-done.5, f32[1536]{0:T(1024)S(1)} %get-tuple-element.79, f32[1536]{0:T(1024)S(1)} %get-tuple-element.98, f32[1536]{0:T(1024)S(1)} %get-tuple-element.106, f32[1536]{0:T(1024)S(1)} %get-tuple-element.105, ...), kind=kLoop, calls=%fused_computation.414 | loop fusion | flops 59609088 | bytes 3962880 | tf_op jit(solution)/shard_map/broadcast_in_dim | solution.py:115
  508.1 211.6 %all-reduce.8.cloned.1.call-done = f32[1536,49]{0,1:T(8,128)} async-done(((f32[1536,49]{0,1:T(8,128)}), f32[1536,49]{0,1:T(8,128)}) %all-reduce.8.cloned.1.call-update) | async-done | bytes 301072
  719.7 0.9 constant_dynamic-slice_fusion
  720.6 0.7 copy.9
  (62 shorter events, 0.4 us)
Async XLA Ops:
  7.2 37.7 %copy-start = (bf16[1536,768]{1,0:T(8,128)(2,1)S(1)}, bf16[1536,768]{1,0:T(8,128)(2,1)}, u32[]{:S(2)}) copy-start(bf16[1536,768]{1,0:T(8,128)(2,1)} %param.8) | copy-start | bytes 7077892
  11.5 32.3 %copy-start.3 = (bf16[1,8,7,7,1536]{4,1,3,2,0:T(8,128)(2,1)S(1)}, bf16[1,8,7,7,1536]{4,1,3,2,0:T(8,128)(2,1)}, u32[]{:S(2)}) copy-start(bf16[1,8,7,7,1536]{4,1,3,2,0:T(8,128)(2,1)} %param.5) | copy-start | bytes 3612676
  43.4 1.5 copy-start.1
  44.9 12.5 %copy-start.6 = (s32[1,256]{1,0:T(1,128)S(1)}, s32[1,256]{1,0:T(1,128)}, u32[]{:S(2)}) copy-start(s32[1,256]{1,0:T(1,128)} %param.6) | copy-start | bytes 3076
  46.3 24.8 %all-to-all-start = ((bf16[32,8,768]{2,1,0:T(8,128)(2,1)}), bf16[32,8,768]{2,1,0:T(8,128)(2,1)S(1)}, u32[]{:S(2)}, u32[]{:S(2)}) async-start(bf16[32,8,768]{2,1,0:T(8,128)(2,1)} %stack.185), calls=%async_computation | async-start | bytes 786432 | tf_op jit(solution)/shard_map/all_to_all | solution.py:82
  57.3 390.1 %all-reduce.6.cloned.1.call-start = ((), (), s32[]{:S(2)}) async-start(), calls=%async_computation.1 | async-start | bytes 1572864 | tf_op jit(solution)/shard_map/psum | solution.py:107
  219.2 500.5 %all-reduce.8.cloned.1.call-start = ((), (), s32[]{:S(2)}) async-start(), calls=%async_computation.2 | async-start | bytes 688128
  447.4 2.8 copy-start.2
  448.5 2.3 copy-start.4
  458.5 2.4 copy-start.5
Sparse Core Ops, SparseCore 0:
  219.4 228.0 all-reduce.5
  469.9 249.7 all-reduce.7
